TPU v7x, 32 devices: a whole 2x2x4 slice. The times are simulated.
32 devices in a mesh: dp: 4 (over z), expert: 8 (over y, x, core).
Axes of the slice: x: 2, y: 2, z: 4, core: 2. Of those that a mesh axis runs over, the one named last changes fastest.
Arguments:
- tokens: bfloat16 [32768, 768], P(('dp', 'expert')), may hold values from -6 to 6
- lengths: int32 [32], P(('dp', 'expert')), may hold values from 128 to 1024, as said below
- expert_index: int32 [32768], P(('dp', 'expert')), may hold values from 0 to 7, as said below
- centroids: float32 [8, 768], replicated, may hold values from -0.15625 to 0.15625
- input_weight: bfloat16 [768, 2304], replicated, may hold values from -0.3125 to 0.3125
- output_weight: bfloat16 [768, 768], replicated, may hold values from -0.875 to 0.875
- first_gain: float32 [768], replicated, may hold values from 0.5 to 1.5
- first_shift: float32 [768], replicated, may hold values from -1 to 1
- second_gain: float32 [768], replicated, may hold values from 0.5 to 1.5
- second_shift: float32 [768], replicated, may hold values from -1 to 1
- up_weight: bfloat16 [8, 768, 3072], P('expert'), may hold values from -0.21875 to 0.21875
- down_weight: bfloat16 [8, 3072, 768], P('expert'), may hold values from -0.3125 to 0.3125
- cotangent: bfloat16 [32768, 768], P(('dp', 'expert')), may hold values from -6 to 6
Outputs:
- layer_output: bfloat16 [32768, 768], P(('dp', 'expert'))
- input_gradient: bfloat16 [32768, 768], P(('dp', 'expert'))
- input_weight_gradient: float32 [768, 2304], P('dp')
- output_weight_gradient: float32 [768, 768], P('dp')
- first_gain_gradient: float32 [768], P('dp')
- first_shift_gradient: float32 [768], P('dp')
- second_gain_gradient: float32 [768], P('dp')
- second_shift_gradient: float32 [768], P('dp')
- up_weight_gradient: float32 [8, 768, 3072], P('expert', 'dp')
- down_weight_gradient: float32 [8, 3072, 768], P('expert', 'dp')
Inputs may be any that keep to these rules, and one draw needn't show every extreme that they name: `lengths`: some sequence has exactly 1024 live positions. `expert_index`: in each aligned block of 1024 rows (the sequences of one device), at most 128 rows inside their sequence's length name any one expert, and one expert, the same in every block, is named by exactly 128 of them.
All inputs are finite; a program needn't handle non-finite values.
Results may differ from a plain program's by a relative error of at most 0.015.
Values may be sent and summed in bfloat16 or wider, within the bound.
No kernel may reach another device: no remote copies, remote signals or barrier semaphores. Data moves between devices by JAX's collectives and lax.ppermute only.
A program may use at most 256 MiB of HBM per device.

v0:
```python
import jax
import jax.numpy as jnp
from jax import lax
from jax.sharding import PartitionSpec as P

HEADS = 12
LEN = 1024
epsilon = 1e-05
excluded = -1e30


def layer_norm(values, norm_gain, norm_shift):
    average = jnp.mean(values, axis=-1, keepdims=True)
    centred = values - average
    variance = jnp.mean(centred * centred, axis=-1, keepdims=True)
    return centred * lax.rsqrt(variance + epsilon) * norm_gain + norm_shift


def exact_gelu(values):
    return jax.nn.gelu(values, approximate=False)


def masked_scores(query_block, key_rows, lengths, first_row, scale_factor):
    scores = (
        jnp.einsum("sqhd,skhd->shqk", query_block, key_rows, preferred_element_type=jnp.float32)
        * scale_factor
    )
    rows = first_row + jnp.arange(query_block.shape[1])
    columns = jnp.arange(key_rows.shape[1])
    causal = columns[None, :] <= rows[:, None]
    inside = columns[None, :] < lengths[:, None]
    allowed = causal[None, None, :, :] & inside[:, None, None, :]
    return jnp.where(allowed, scores, excluded)


def on_device(
    tokens,
    lengths,
    expert_index,
    centroids,
    input_weight,
    output_weight,
    first_gain,
    first_shift,
    second_gain,
    second_shift,
    up_weight,
    down_weight,
    cotangent,
):
    row_count = tokens.shape[0]
    width = tokens.shape[1]
    sequences = lengths.shape[0]
    experts = centroids.shape[0]
    capacity = row_count // experts
    head_size = width // HEADS
    block = min(512, LEN)
    scale_factor = head_size ** (-0.5)
    split_heads = (sequences, LEN, HEADS, head_size)
    positions = jnp.arange(row_count)
    present = positions % LEN < jnp.repeat(lengths, LEN)
    row_mask = present.astype(jnp.float32)[:, None]
    inputs_float = tokens.astype(jnp.float32)
    normed, first_back = jax.vjp(layer_norm, inputs_float, first_gain, first_shift)
    normed_low = normed.astype(jnp.bfloat16)
    projected = jnp.dot(normed_low, input_weight, preferred_element_type=jnp.float32)
    queries = projected[:, :width].astype(jnp.bfloat16).reshape(split_heads)
    keys = projected[:, width : 2 * width].astype(jnp.bfloat16).reshape(split_heads)
    values = projected[:, 2 * width :].astype(jnp.bfloat16).reshape(split_heads)
    mixed_blocks = []
    kept_top = []
    kept_total = []
    for first_row in range(0, LEN, block):
        upto = first_row + block
        scores = masked_scores(
            queries[:, first_row:upto], keys[:, :upto], lengths, first_row, scale_factor
        )
        top = jnp.max(scores, axis=-1, keepdims=True)
        weights = jnp.exp(scores - top)
        total = jnp.sum(weights, axis=-1, keepdims=True)
        probs_low = (weights / total).astype(jnp.bfloat16)
        mixed_blocks.append(
            jnp.einsum(
                "shqk,skhd->sqhd", probs_low, values[:, :upto], preferred_element_type=jnp.float32
            )
        )
        kept_top.append(top)
        kept_total.append(total)
    mixed_low = jnp.concatenate(mixed_blocks, axis=1).reshape(row_count, width).astype(jnp.bfloat16)
    branch = jnp.dot(mixed_low, output_weight, preferred_element_type=jnp.float32)
    residual = inputs_float + row_mask * branch
    hidden, second_back = jax.vjp(layer_norm, residual, second_gain, second_shift)
    hidden_low = hidden.astype(jnp.bfloat16)
    onehot = expert_index[:, None] == jnp.arange(experts)[None, :]
    picked = jnp.dot(
        onehot.astype(jnp.float32),
        centroids,
        precision=lax.Precision.HIGHEST,
        preferred_element_type=jnp.float32,
    )
    gate = jax.nn.sigmoid(jnp.sum(hidden * picked, axis=-1))
    routed = onehot & present[:, None]
    counts = jnp.cumsum(routed.astype(jnp.int32), axis=0)
    slot = jnp.sum(jnp.where(routed, counts - 1, 0), axis=1)
    target = jnp.where(present, expert_index * capacity + slot, experts * capacity)
    outgoing = (
        jnp.zeros((experts * capacity, width), jnp.bfloat16)
        .at[target]
        .set(hidden_low, mode="drop")
        .reshape(experts, capacity, width)
    )
    arrived = lax.all_to_all(outgoing, "expert", split_axis=0, concat_axis=0, tiled=True)
    count = arrived.shape[1]
    flat = arrived.reshape(-1, width)
    upper = jnp.dot(flat, up_weight[0], preferred_element_type=jnp.float32)
    expert_active = exact_gelu(upper).astype(jnp.bfloat16)
    produced = jnp.dot(expert_active, down_weight[0], preferred_element_type=jnp.float32).astype(
        jnp.bfloat16
    )
    returned = lax.all_to_all(
        produced.reshape(experts, count, width), "expert", split_axis=0, concat_axis=0, tiled=True
    )
    results = (returned, arrived)
    returned = results[0]
    arrived = results[1]
    expert_term = jnp.take(
        returned.reshape(experts * capacity, width), target, axis=0, mode="fill", fill_value=0
    ).astype(jnp.float32)
    scaled = row_mask * gate[:, None]
    layer_output = (residual + scaled * expert_term).astype(jnp.bfloat16)
    upstream = cotangent.astype(jnp.float32)
    produced_gradient = (scaled * upstream).astype(jnp.bfloat16)
    logit_gradient = row_mask[:, 0] * jnp.sum(upstream * expert_term, axis=-1) * gate * (1.0 - gate)
    gradient_outgoing = (
        jnp.zeros((experts * capacity, width), jnp.bfloat16)
        .at[target]
        .set(produced_gradient, mode="drop")
        .reshape(experts, capacity, width)
    )
    arrived_gradient = lax.all_to_all(
        gradient_outgoing, "expert", split_axis=0, concat_axis=0, tiled=True
    ).reshape(-1, width)
    arrived_rows = arrived.reshape(-1, width)
    upper = jnp.dot(arrived_rows, up_weight[0], preferred_element_type=jnp.float32)
    active_float, gelu_back = jax.vjp(exact_gelu, upper)
    active = active_float.astype(jnp.bfloat16)
    dp_count = lax.axis_size("dp")
    part = active
    down_weight_gradient = lax.psum_scatter(
        jnp.einsum("rf,rd->fd", part, arrived_gradient, preferred_element_type=jnp.float32).astype(
            jnp.bfloat16
        ),
        "dp",
        scatter_dimension=0,
        tiled=True,
    ).astype(jnp.float32)
    active_gradient = jnp.einsum(
        "rd,fd->rf", arrived_gradient, down_weight[0], preferred_element_type=jnp.float32
    )
    upper_gradient = gelu_back(active_gradient)[0].astype(jnp.bfloat16)
    part = arrived_rows
    up_weight_gradient = lax.psum_scatter(
        jnp.einsum("rd,rf->df", part, upper_gradient, preferred_element_type=jnp.float32).astype(
            jnp.bfloat16
        ),
        "dp",
        scatter_dimension=0,
        tiled=True,
    ).astype(jnp.float32)
    sent_back = jnp.einsum(
        "rf,df->rd", upper_gradient, up_weight[0], preferred_element_type=jnp.float32
    ).astype(jnp.bfloat16)
    hidden_back = lax.all_to_all(
        sent_back.reshape(experts, capacity, width),
        "expert",
        split_axis=0,
        concat_axis=0,
        tiled=True,
    )
    expert_hidden = jnp.take(
        hidden_back.reshape(experts * capacity, width), target, axis=0, mode="fill", fill_value=0
    ).astype(jnp.float32)
    hidden_gradient = expert_hidden + logit_gradient[:, None] * picked
    residual_part, second_gain_gradient, second_shift_gradient = second_back(hidden_gradient)
    residual_gradient = upstream + residual_part
    branch_gradient = (row_mask * residual_gradient).astype(jnp.bfloat16)
    output_weight_gradient = jnp.einsum(
        "rd,re->de", mixed_low, branch_gradient, preferred_element_type=jnp.float32
    )
    mixed_gradient = (
        jnp.einsum("re,de->rd", branch_gradient, output_weight, preferred_element_type=jnp.float32)
        .astype(jnp.bfloat16)
        .reshape(split_heads)
    )
    query_blocks = []
    key_gradient = jnp.zeros(split_heads, jnp.float32)
    value_gradient = jnp.zeros(split_heads, jnp.float32)
    for number, first_row in enumerate(range(0, LEN, block)):
        upto = first_row + block
        query_block = queries[:, first_row:upto]
        scores = masked_scores(query_block, keys[:, :upto], lengths, first_row, scale_factor)
        probs = jnp.exp(scores - kept_top[number]) / kept_total[number]
        probs_low = probs.astype(jnp.bfloat16)
        incoming = mixed_gradient[:, first_row:upto]
        prob_gradient = jnp.einsum(
            "sqhd,skhd->shqk", incoming, values[:, :upto], preferred_element_type=jnp.float32
        )
        inner = jnp.sum(probs * prob_gradient, axis=-1, keepdims=True)
        score_gradient = (probs * (prob_gradient - inner)).astype(jnp.bfloat16)
        query_blocks.append(
            jnp.einsum(
                "shqk,skhd->sqhd",
                score_gradient,
                keys[:, :upto],
                preferred_element_type=jnp.float32,
            )
            * scale_factor
        )
        key_gradient = key_gradient.at[:, :upto].add(
            jnp.einsum(
                "shqk,sqhd->skhd", score_gradient, query_block, preferred_element_type=jnp.float32
            )
            * scale_factor
        )
        value_gradient = value_gradient.at[:, :upto].add(
            jnp.einsum("shqk,sqhd->skhd", probs_low, incoming, preferred_element_type=jnp.float32)
        )
    query_gradient = jnp.concatenate(query_blocks, axis=1)
    projected_gradient = jnp.concatenate(
        [
            query_gradient.reshape(row_count, width),
            key_gradient.reshape(row_count, width),
            value_gradient.reshape(row_count, width),
        ],
        axis=1,
    ).astype(jnp.bfloat16)
    input_weight_gradient = jnp.einsum(
        "rd,re->de", normed_low, projected_gradient, preferred_element_type=jnp.float32
    )
    normed_gradient = jnp.einsum(
        "re,de->rd", projected_gradient, input_weight, preferred_element_type=jnp.float32
    )
    input_part, first_gain_gradient, first_shift_gradient = first_back(normed_gradient)
    input_gradient = (residual_gradient + input_part).astype(jnp.bfloat16)
    gain_columns = jnp.stack(
        [first_gain_gradient, first_shift_gradient, second_gain_gradient, second_shift_gradient],
        axis=1,
    )
    total_input, total_output, total_gains = lax.psum(
        (input_weight_gradient, output_weight_gradient, gain_columns), ("dp", "expert")
    )
    share = width // dp_count
    begin = lax.axis_index("dp") * share
    input_share = lax.dynamic_slice_in_dim(total_input, begin, share, 0)
    output_share = lax.dynamic_slice_in_dim(total_output, begin, share, 0)
    gain_share = lax.dynamic_slice_in_dim(total_gains, begin, share, 0)
    return (
        layer_output,
        input_gradient,
        input_share,
        output_share,
        gain_share[:, 0],
        gain_share[:, 1],
        gain_share[:, 2],
        gain_share[:, 3],
        up_weight_gradient[None],
        down_weight_gradient[None],
    )


def solution(mesh):
    return jax.shard_map(
        on_device,
        mesh=mesh,
        in_specs=(
            P(("dp", "expert"), None),
            P(("dp", "expert")),
            P(("dp", "expert")),
            P(),
            P(),
            P(),
            P(),
            P(),
            P(),
            P(),
            P("expert", None, None),
            P("expert", None, None),
            P(("dp", "expert"), None),
        ),
        out_specs=(
            P(("dp", "expert"), None),
            P(("dp", "expert"), None),
            P("dp", None),
            P("dp", None),
            P("dp"),
            P("dp"),
            P("dp"),
            P("dp"),
            P("expert", "dp", None),
            P("expert", "dp", None),
        ),
        check_vma=False,
    )
```

profile of v0, /device:TPU:0, one launch (start us, length us, event | category | flops | bytes accessed | tf_op | source)
XLA Modules:
  0.0 812.4 jit_solution(16364089621944587762)
XLA Ops:
  43.2 13.4 %fusion.85 = f32[12,512,1024]{2,1,0:T(8,128)} fusion(bf16[1024,12,64]{0,2,1:T(8,128)(2,1)} %bitcast.177, bf16[1,1024,12,64]{1,3,2,0:T(8,128)(2,1)} %bitcast.181), kind=kOutput, calls=%fused_computation.133 | convolution fusion | flops 805306368 | bytes 27525120 | tf_op jit(solution)/shard_map/sqhd,skhd->shqk/dot_general | solution.py:25
  56.6 11.1 %fusion.121 = (f32[12,512]{1,0:T(8,128)}, f32[12,512,512]{1,2,0:T(8,128)}) fusion(pred[512,512]{0,1:T(8,128)(4,1)} %fusion.79, bf16[1,1024,12,64]{1,3,2,0:T(8,128)(2,1)} %bitcast.182, bf16[1,1024,12,64]{1,3,2,0:T(8,128)(2,1)} %bitcast.178), kind=kOutput, calls=%fused_computation.196 | convolution fusion | flops 415236608 | bytes 14442496 | tf_op jit(solution)/shard_map/sub | solution.py:79
  67.7 34.4 %fusion.120 = (f32[12,512]{1,0:T(8,128)}, f32[12,512,1024]{2,1,0:T(8,128)}) fusion(f32[12,512,1024]{2,1,0:T(8,128)} %fusion.85, pred[512,1024]{1,0:T(8,128)(4,1)} %fusion.49), kind=kOutput, calls=%fused_computation.195 | output fusion | flops 37749760 | bytes 50880512 | tf_op jit(solution)/shard_map/sub | solution.py:79
  108.1 10.3 %fusion.71 = bf16[1,512,12,64]{1,3,2,0:T(8,128)(2,1)S(1)} fusion(bf16[1024,12,64]{0,2,1:T(8,128)(2,1)S(1)} %bitcast.195, f32[12,512,1024]{2,1,0:T(8,128)} %get-tuple-element.121, f32[12,512]{1,0:T(8,128)S(1)} %copy-done.50), kind=kOutput, calls=%fused_computation.114 | convolution fusion | flops 818282496 | bytes 27549696 | tf_op jit(solution)/shard_map/shqk,skhd->sqhd/dot_general | solution.py:83
  139.2 26.6 %all_to_all.20 = bf16[8,128,768]{2,1,0:T(8,128)(2,1)S(1)} all-to-all(bf16[8,128,768]{2,1,0:T(8,128)(2,1)} %bitcast.188), channel_id=1, replica_groups=mesh['dp'=4,'expert'=8] {'expert'}, dimensions={0} | all-to-all | bytes 3145728 | tf_op jit(solution)/shard_map/all_to_all | solution.py:112
  165.8 35.7 %multiply_convert_fusion.2 = (bf16[1024,3072]{1,0:T(8,128)(2,1)S(1)}, f32[1024,3072]{1,0:T(8,128)}, f32[1024,3072]{1,0:T(8,128)}) fusion(bf16[1024,768]{1,0:T(8,128)(2,1)S(1)} %bitcast.191, bf16[1,768,3072]{2,1,0:T(8,128)(2,1)} %param.37), kind=kOutput, calls=%fused_computation.16 | convolution fusion | flops 5036310528 | bytes 37748736 | tf_op jit(solution)/shard_map/dot_general | solution.py:115
  201.5 10.7 %fusion.57 = bf16[1024,768]{1,0:T(8,128)(2,1)} fusion(bf16[1024,3072]{1,0:T(8,128)(2,1)S(1)} %get-tuple-element.106, bf16[1,3072,768]{2,1,0:T(8,128)(2,1)} %param.38), kind=kOutput, calls=%fused_computation.102 | convolution fusion | flops 4832624640 | bytes 12582912 | tf_op jit(solution)/shard_map/dot_general | solution.py:117
  219.2 18.4 %all-to-all-done.1 = bf16[8,128,768]{2,1,0:T(8,128)(2,1)} async-done(((bf16[8,128,768]{2,1,0:T(8,128)(2,1)}), bf16[8,128,768]{2,1,0:T(8,128)(2,1)}, u32[]{:S(2)}, u32[]{:S(2)}) %all-to-all-start.1) | async-done | bytes 1572896 | tf_op jit(solution)/shard_map/all_to_all | solution.py:120
  237.6 7.2 gather_fusion
  261.4 24.7 %all_to_all.21 = bf16[8,128,768]{2,1,0:T(8,128)(2,1)S(1)} all-to-all(bf16[8,128,768]{2,1,0:T(8,128)(2,1)} %bitcast.187), channel_id=1, replica_groups=mesh['dp'=4,'expert'=8] {'expert'}, dimensions={0} | all-to-all | bytes 3145728 | tf_op jit(solution)/shard_map/all_to_all | solution.py:140
  286.0 16.4 %add_convert_fusion = bf16[1024,3072]{1,0:T(8,128)(2,1)} fusion(f32[1024,3072]{1,0:T(8,128)} %get-tuple-element.107, f32[1024,3072]{1,0:T(8,128)} %get-tuple-element.127, bf16[1024,768]{1,0:T(8,128)(2,1)S(1)} %bitcast.199, bf16[1,3072,768]{2,1,0:T(8,128)(2,1)} %param.38), kind=kOutput, calls=%fused_computation.15 | convolution fusion | flops 4875878400 | bytes 37748736 | tf_op jit(solution)/shard_map/rd,fd->rf/dot_general | solution.py:157
  302.4 9.5 %fusion.54 = bf16[1024,768]{1,0:T(8,128)(2,1)} fusion(bf16[1024,3072]{1,0:T(8,128)(2,1)} %add_convert_fusion, bf16[1,768,3072]{2,1,0:T(8,128)(2,1)} %param.37), kind=kOutput, calls=%fused_computation.101 | convolution fusion | flops 4832624640 | bytes 12582912 | tf_op jit(solution)/shard_map/rf,df->rd/dot_general | solution.py:170
  316.4 21.0 %all-to-all-done.3 = bf16[8,128,768]{2,1,0:T(8,128)(2,1)} async-done(((bf16[8,128,768]{2,1,0:T(8,128)(2,1)}), bf16[8,128,768]{2,1,0:T(8,128)(2,1)}, u32[]{:S(2)}, u32[]{:S(2)}) %all-to-all-start.3) | async-done | bytes 1572896 | tf_op jit(solution)/shard_map/all_to_all | solution.py:173
  337.3 7.2 gather_fusion.1
  385.9 17.8 %multiply_reduce_fusion = (f32[12,512]{1,0:T(8,128)}, f32[12,512,1024]{2,1,0:T(8,128)}) fusion(f32[12,512,1024]{2,1,0:T(8,128)} %get-tuple-element.121, f32[12,512]{1,0:T(8,128)} %get-tuple-element.120, bf16[1024,12,64]{0,2,1:T(8,128)(2,1)} %bitcast.194, bf16[1,1024,12,64]{1,3,2,0:T(8,128)(2,1)} %bitcast.215), kind=kOutput, calls=%fused_computation.7 | convolution fusion | flops 824174592 | bytes 52748288 | tf_op jit(solution)/shard_map/sqhd,skhd->shqk/dot_general | solution.py:205
  403.7 10.6 %fusion.42 = bf16[1,1024,12,64]{1,3,2,0:T(8,128)(2,1)S(1)} fusion(f32[1,512,12,64]{1,3,2,0:T(8,128)} %fusion.60, bf16[1,1024,12,64]{1,3,2,0:T(8,128)(2,1)} %bitcast.216, f32[12,512,1024]{2,1,0:T(8,128)} %get-tuple-element.121, f32[12,512]{1,0:T(8,128)} %get-tuple-element.120), kind=kOutput, calls=%fused_computation.81 | convolution fusion | flops 819462144 | bytes 29130752 | tf_op jit(solution)/shard_map/shqk,sqhd->skhd/dot_general | solution.py:226
  414.4 21.8 %multiply_convert_fusion = bf16[12,512,1024]{2,1,0:T(8,128)(2,1)} fusion(f32[12,512,1024]{2,1,0:T(8,128)} %get-tuple-element.131, f32[12,512]{1,0:T(8,128)S(1)} %copy-done.52, f32[12,512,1024]{2,1,0:T(8,128)} %get-tuple-element.121, f32[12,512]{1,0:T(8,128)S(1)} %copy-done.51), kind=kLoop, calls=%fused_computation.6 | loop fusion | flops 25165824 | bytes 62963712 | tf_op jit(solution)/shard_map/convert_element_type | solution.py:209
  436.2 8.6 %fusion.77 = bf16[1,512,12,64]{1,3,2,0:T(8,128)(2,1)S(1)} fusion(bf16[1024,12,64]{0,2,1:T(8,128)(2,1)S(1)} %bitcast.180, bf16[12,512,1024]{2,1,0:T(8,128)(2,1)} %multiply_convert_fusion), kind=kOutput, calls=%fused_computation.116 | convolution fusion | flops 806092800 | bytes 14942208 | tf_op jit(solution)/shard_map/shqk,skhd->sqhd/dot_general | solution.py:211
  454.4 7.1 fusion.50
  461.5 9.1 %convolution_convert_fusion.1 = bf16[3072,768]{1,0:T(8,128)(2,1)} fusion(bf16[1024,3072]{1,0:T(8,128)(2,1)} %copy-done.72, bf16[1024,768]{1,0:T(8,128)(2,1)} %bitcast.200), kind=kOutput, calls=%fused_computation.46 | convolution fusion | flops 4834197504 | bytes 12582912 | tf_op jit(solution)/shard_map/rf,rd->fd/dot_general | solution.py:150
  470.8 9.5 %convolution_convert_fusion.2 = bf16[768,3072]{1,0:T(8,128)(2,1)} fusion(bf16[1024,768]{1,0:T(8,128)(2,1)} %bitcast.192, bf16[1024,3072]{1,0:T(8,128)(2,1)} %add_convert_fusion), kind=kOutput, calls=%fused_computation.47 | convolution fusion | flops 4834197504 | bytes 12582912 | tf_op jit(solution)/shard_map/rd,rf->df/dot_general | solution.py:163
  484.7 7.9 fusion.123
  508.8 43.2 %psum.23 = f32[768,4]{0,1:T(4,128)} all-reduce(f32[768,4]{0,1:T(4,128)S(1)} %pad_maximum_fusion.5), channel_id=1, replica_groups=mesh['dp'=4,'expert'=8] {'dp','expert'}, use_global_device_ids=true, to_apply=%region_27.29 | all-reduce | flops 3072 | bytes 24576 | tf_op jit(solution)/shard_map/psum | solution.py:249
  553.4 240.9 %all-reduce.5.cloned.1.call-done = (f32[768,2304]{1,0:T(8,128)}, f32[768,768]{1,0:T(8,128)}) async-done(((f32[768,2304]{1,0:T(8,128)}, f32[768,768]{1,0:T(8,128)}), (f32[768,2304]{1,0:T(8,128)}, f32[768,768]{1,0:T(8,128)})) %all-reduce.5.cloned.1.call-update) | async-done | bytes 9437200 | tf_op jit(solution)/shard_map/psum | solution.py:249
  (237 shorter events, 172.1 us)
Async XLA Ops:
  8.0 19.3 %copy-start = (bf16[768,2304]{1,0:T(8,128)(2,1)S(1)}, bf16[768,2304]{1,0:T(8,128)(2,1)}, u32[]{:S(2)}) copy-start(bf16[768,2304]{1,0:T(8,128)(2,1)} %param.31) | copy-start | bytes 10616836
  9.9 108.8 %copy-start.56 = (f32[1024]{0:T(1024)}, f32[1024]{0:T(1024)S(1)}, u32[]{:S(2)}) copy-start(f32[1024]{0:T(1024)S(1)} %fusion.106) | copy-start | bytes 12292
  20.4 6.9 copy-start.68
  24.9 6.9 copy-start.30
  132.2 69.3 %copy-start.58 = (s32[1024]{0:T(1024)}, s32[1024]{0:T(1024)S(1)}, u32[]{:S(2)}) copy-start(s32[1024]{0:T(1024)S(1)} %get-tuple-element.105) | copy-start | bytes 12292
  165.8 35.7 %copy-start.21 = (bf16[8,128,768]{2,1,0:T(8,128)(2,1)}, bf16[8,128,768]{2,1,0:T(8,128)(2,1)S(1)}, u32[]{:S(2)}) copy-start(bf16[8,128,768]{2,1,0:T(8,128)(2,1)S(1)} %all_to_all.20) | copy-start | bytes 4718596
  201.5 10.7 %copy-start.72 = (bf16[1024,3072]{1,0:T(8,128)(2,1)}, bf16[1024,3072]{1,0:T(8,128)(2,1)S(1)}, u32[]{:S(2)}) copy-start(bf16[1024,3072]{1,0:T(8,128)(2,1)S(1)} %get-tuple-element.106) | copy-start | bytes 18874372
  212.2 6.9 copy-start.59
  212.2 6.9 copy-start.45
  212.2 25.4 %all-to-all-start.1 = ((bf16[8,128,768]{2,1,0:T(8,128)(2,1)}), bf16[8,128,768]{2,1,0:T(8,128)(2,1)}, u32[]{:S(2)}, u32[]{:S(2)}) async-start(bf16[8,128,768]{2,1,0:T(8,128)(2,1)} %bitcast.204), calls=%async_computation.1 | async-start | bytes 3145728 | tf_op jit(solution)/shard_map/all_to_all | solution.py:120
  219.1 28.2 %copy-start.48 = (f32[1024]{0:T(1024)}, f32[1024]{0:T(1024)S(1)}, u32[]{:S(2)}) copy-start(f32[1024]{0:T(1024)S(1)} %broadcast_select_fusion.1) | copy-start | bytes 12292
  286.0 16.4 %copy-start.26 = (bf16[8,128,768]{2,1,0:T(8,128)(2,1)}, bf16[8,128,768]{2,1,0:T(8,128)(2,1)S(1)}, u32[]{:S(2)}) copy-start(bf16[8,128,768]{2,1,0:T(8,128)(2,1)S(1)} %all_to_all.21) | copy-start | bytes 4718596
  311.9 25.5 %all-to-all-start.3 = ((bf16[8,128,768]{2,1,0:T(8,128)(2,1)}), bf16[8,128,768]{2,1,0:T(8,128)(2,1)}, u32[]{:S(2)}, u32[]{:S(2)}) async-start(bf16[8,128,768]{2,1,0:T(8,128)(2,1)} %bitcast.203), calls=%async_computation.3 | async-start | bytes 3145728 | tf_op jit(solution)/shard_map/all_to_all | solution.py:173
  316.3 478.0 %all-reduce.5.cloned.1.call-start = ((), (), s32[]{:S(2)}) async-start(), calls=%async_computation.8 | async-start | bytes 18874368 | tf_op jit(solution)/shard_map/psum | solution.py:249
  373.8 6.9 copy-start.8
  403.7 10.6 %copy-start.51 = (f32[12,512]{1,0:T(8,128)S(1)}, f32[12,512]{1,0:T(8,128)}, u32[]{:S(2)}) copy-start(f32[12,512]{1,0:T(8,128)} %get-tuple-element.120) | copy-start | bytes 73732
  403.7 10.6 %copy-start.52 = (f32[12,512]{1,0:T(8,128)S(1)}, f32[12,512]{1,0:T(8,128)}, u32[]{:S(2)}) copy-start(f32[12,512]{1,0:T(8,128)} %get-tuple-element.130) | copy-start | bytes 73732
  414.3 37.8 %copy-start.70 = (bf16[1,1024,12,64]{1,3,2,0:T(8,128)(2,1)}, bf16[1,1024,12,64]{1,3,2,0:T(8,128)(2,1)S(1)}, u32[]{:S(2)}) copy-start(bf16[1,1024,12,64]{1,3,2,0:T(8,128)(2,1)S(1)} %fusion.42) | copy-start | bytes 4718596
  414.3 21.9 %copy-start.9 = (bf16[1024,768]{0,1:T(8,128)(2,1)S(1)}, bf16[1024,768]{0,1:T(8,128)(2,1)}, u32[]{:S(2)}) copy-start(bf16[1024,768]{0,1:T(8,128)(2,1)} %copy.46) | copy-start | bytes 4718596
  436.2 8.7 %copy-start.16 = (bf16[1024,768]{0,1:T(8,128)(2,1)S(1)}, bf16[1024,768]{0,1:T(8,128)(2,1)}, u32[]{:S(2)}) copy-start(bf16[1024,768]{0,1:T(8,128)(2,1)} %copy.45) | copy-start | bytes 4718596
  436.2 8.7 %copy-start.18 = (f32[1,512,12,64]{1,3,2,0:T(8,128)S(1)}, f32[1,512,12,64]{1,3,2,0:T(8,128)}, u32[]{:S(2)}) copy-start(f32[1,512,12,64]{1,3,2,0:T(8,128)} %multiply_bitcast_fusion) | copy-start | bytes 4718596
  444.9 7.0 copy-start.20
  461.5 337.5 %reduce-scatter.5.cloned.1.call-start = ((), (), s32[]{:S(2)}) async-start(), calls=%async_computation.7 | async-start | bytes 5898240 | tf_op jit(solution)/shard_map/reduce_scatter | solution.py:149
  470.7 331.2 %reduce-scatter.3.cloned.1.call-start = ((), (), s32[]{:S(2)}) async-start(), calls=%async_computation.6 | async-start | bytes 5898240 | tf_op jit(solution)/shard_map/reduce_scatter | solution.py:162
  (57 other events, 194.5 us)
Sparse Core Ops, SparseCore 0:
  461.6 332.6 all-reduce.4
Sparse Core Ops, SparseCore 1:
  470.8 99.6 reduce-scatter.4
  572.8 97.5 reduce-scatter.2
where the time goes:
time: 818 us; the launch traced here: 812 us
  waiting for transfers between devices  280 us (34%)
  matrix products  220 us (27%)
  other arithmetic  109 us (13%)
  blocking collectives  94.5 us (12%)
  local copies, waits for them, and re-layouts  82.5 us (10%)
  between operations  17.3 us (2%)
  starting transfers between devices  8.87 us (1%)
    psum x1, waiting for transfers between devices, on_device(): lax.psum((input_weight_gradient, output_weight_gradient, gain_columns), (...  241 us
    psum x1, blocking collectives, on_device(): lax.psum((input_weight_gradient, output_weight_gradient, gain_columns), (...  43.2 us
    dot_general x1, matrix products, on_device(): upper = jnp.dot(flat, up_weight[0], preferred_element_type=jnp.float32)  35.7 us
    sub x1, other arithmetic, on_device(): weights = jnp.exp(scores - top)  34.4 us
    convert_element_type x2, other arithmetic, on_device(): score_gradient = (probs * (prob_gradient - inner)).astype(jnp.bfloat16)  28.8 us
    all_to_all x1, blocking collectives, on_device(): lax.all_to_all(outgoing, 'expert', split_axis=0, concat_axis=0, tiled=True)  26.6 us
    all_to_all x1, blocking collectives, on_device(): lax.all_to_all(gradient_outgoing, 'expert', split_axis=0, concat_axis=0,...  24.7 us
    dot_general x2, matrix products, on_device(): jnp.einsum('sqhd,skhd->shqk', incoming, values[:, :upto], preferred_eleme...  23.5 us
  transfers between devices with their start and end apart: 5, of which 3 were waited for; matrix products, arithmetic and copies ran while one was open for 7% of the time, Pallas kernels for 0%

commit v1 on v0

--- a/solution.py
+++ b/solution.py
@@ -1,3 +1,4 @@
+import functools
 import jax
 import jax.numpy as jnp
 from jax import lax
@@ -7,6 +8,14 @@
 LEN = 1024
 epsilon = 1e-05
 excluded = -1e30
+
+
+def thing_lay(panel, mesh_name, shard_axis):
+    current_value = lax.psum(panel, mesh_name)
+    return lax.psum(current_value, shard_axis)
+
+
+pair_tokens = functools.partial(thing_lay, mesh_name="expert", shard_axis="dp")
 
 
 def layer_norm(values, norm_gain, norm_shift):
@@ -246,8 +255,8 @@
         [first_gain_gradient, first_shift_gradient, second_gain_gradient, second_shift_gradient],
         axis=1,
     )
-    total_input, total_output, total_gains = lax.psum(
-        (input_weight_gradient, output_weight_gradient, gain_columns), ("dp", "expert")
+    total_input, total_output, total_gains = pair_tokens(
+        (input_weight_gradient, output_weight_gradient, gain_columns)
     )
     share = width // dp_count
     begin = lax.axis_index("dp") * share

time: 818 us -> 990 us (1.21)
  waiting for transfers between devices: 280 us -> 452 us
    psum x1 -> x2, waiting for transfers between devices: 241 us -> 413 us  [the longest x1 294 us: thing_lay(): return lax.psum(current_value, shard_axis)]
    psum x1 -> x2, blocking collectives: 43.2 us -> 44.2 us  [the longest x1 23.4 us: thing_lay(): current_value = lax.psum(panel, mesh_name)]
  transfers between devices with their start and end apart: 5 -> 6, of which waited for: 3 -> 4; matrix products, arithmetic and copies ran while one was open for 7% -> 6% of each run, Pallas kernels for 0% -> 0%
where the time goes in v1:
time: 990 us; the launch traced here: 984 us
  waiting for transfers between devices  452 us (46%)
  matrix products  220 us (22%)
  other arithmetic  109 us (11%)
  blocking collectives  95.5 us (10%)
  local copies, waits for them, and re-layouts  81.5 us (8%)
  between operations  17.5 us (2%)
    psum x1, waiting for transfers between devices, thing_lay(): return lax.psum(current_value, shard_axis)  294 us
    psum x1, waiting for transfers between devices, thing_lay(): current_value = lax.psum(panel, mesh_name)  119 us
    dot_general x1, matrix products, on_device(): upper = jnp.dot(flat, up_weight[0], preferred_element_type=jnp.float32)  35.7 us
    sub x1, other arithmetic, on_device(): weights = jnp.exp(scores - top)  34.3 us
    convert_element_type x2, other arithmetic, on_device(): score_gradient = (probs * (prob_gradient - inner)).astype(jnp.bfloat16)  28.8 us
    all_to_all x1, blocking collectives, on_device(): lax.all_to_all(outgoing, 'expert', split_axis=0, concat_axis=0, tiled=True)  26.6 us
    all_to_all x1, blocking collectives, on_device(): lax.all_to_all(gradient_outgoing, 'expert', split_axis=0, concat_axis=0,...  24.7 us
    dot_general x2, matrix products, on_device(): jnp.einsum('sqhd,skhd->shqk', incoming, values[:, :upto], preferred_eleme...  23.5 us
  transfers between devices with their start and end apart: 6, of which 4 were waited for; matrix products, arithmetic and copies ran while one was open for 6% of the time, Pallas kernels for 0%

profile of v1, /device:TPU:0, one launch (start us, length us, event | category | flops | bytes accessed | tf_op | source)
XLA Modules:
  0.0 984.3 jit_solution(482732953064682736)
XLA Ops:
  43.2 13.4 %fusion.85 = f32[12,512,1024]{2,1,0:T(8,128)} fusion(bf16[1024,12,64]{0,2,1:T(8,128)(2,1)} %bitcast.177, bf16[1,1024,12,64]{1,3,2,0:T(8,128)(2,1)} %bitcast.181), kind=kOutput, calls=%fused_computation.133 | convolution fusion | flops 805306368 | bytes 27525120 | tf_op jit(solution)/shard_map/sqhd,skhd->shqk/dot_general | solution.py:34
  56.6 11.1 %fusion.121 = (f32[12,512]{1,0:T(8,128)}, f32[12,512,512]{1,2,0:T(8,128)}) fusion(pred[512,512]{0,1:T(8,128)(4,1)} %fusion.79, bf16[1,1024,12,64]{1,3,2,0:T(8,128)(2,1)} %bitcast.182, bf16[1,1024,12,64]{1,3,2,0:T(8,128)(2,1)} %bitcast.178), kind=kOutput, calls=%fused_computation.196 | convolution fusion | flops 415236608 | bytes 14442496 | tf_op jit(solution)/shard_map/sub | solution.py:88
  67.6 34.3 %fusion.120 = (f32[12,512]{1,0:T(8,128)}, f32[12,512,1024]{2,1,0:T(8,128)}) fusion(f32[12,512,1024]{2,1,0:T(8,128)} %fusion.85, pred[512,1024]{1,0:T(8,128)(4,1)} %fusion.49), kind=kOutput, calls=%fused_computation.195 | output fusion | flops 37749760 | bytes 50880512 | tf_op jit(solution)/shard_map/sub | solution.py:88
  108.0 10.3 %fusion.71 = bf16[1,512,12,64]{1,3,2,0:T(8,128)(2,1)S(1)} fusion(bf16[1024,12,64]{0,2,1:T(8,128)(2,1)S(1)} %bitcast.195, f32[12,512,1024]{2,1,0:T(8,128)} %get-tuple-element.123, f32[12,512]{1,0:T(8,128)S(1)} %copy-done.50), kind=kOutput, calls=%fused_computation.114 | convolution fusion | flops 818282496 | bytes 27549696 | tf_op jit(solution)/shard_map/shqk,skhd->sqhd/dot_general | solution.py:92
  139.1 26.6 %all_to_all.20 = bf16[8,128,768]{2,1,0:T(8,128)(2,1)S(1)} all-to-all(bf16[8,128,768]{2,1,0:T(8,128)(2,1)} %bitcast.188), channel_id=1, replica_groups=mesh['dp'=4,'expert'=8] {'expert'}, dimensions={0} | all-to-all | bytes 3145728 | tf_op jit(solution)/shard_map/all_to_all | solution.py:121
  165.7 35.7 %multiply_convert_fusion.2 = (bf16[1024,3072]{1,0:T(8,128)(2,1)S(1)}, f32[1024,3072]{1,0:T(8,128)}, f32[1024,3072]{1,0:T(8,128)}) fusion(bf16[1024,768]{1,0:T(8,128)(2,1)S(1)} %bitcast.191, bf16[1,768,3072]{2,1,0:T(8,128)(2,1)} %param.37), kind=kOutput, calls=%fused_computation.16 | convolution fusion | flops 5036310528 | bytes 37748736 | tf_op jit(solution)/shard_map/dot_general | solution.py:124
  201.4 10.7 %fusion.57 = bf16[1024,768]{1,0:T(8,128)(2,1)} fusion(bf16[1024,3072]{1,0:T(8,128)(2,1)S(1)} %get-tuple-element.108, bf16[1,3072,768]{2,1,0:T(8,128)(2,1)} %param.38), kind=kOutput, calls=%fused_computation.102 | convolution fusion | flops 4832624640 | bytes 12582912 | tf_op jit(solution)/shard_map/dot_general | solution.py:126
  219.1 18.4 %all-to-all-done.1 = bf16[8,128,768]{2,1,0:T(8,128)(2,1)} async-done(((bf16[8,128,768]{2,1,0:T(8,128)(2,1)}), bf16[8,128,768]{2,1,0:T(8,128)(2,1)}, u32[]{:S(2)}, u32[]{:S(2)}) %all-to-all-start.1) | async-done | bytes 1572896 | tf_op jit(solution)/shard_map/all_to_all | solution.py:129
  237.5 7.2 gather_fusion
  261.3 24.7 %all_to_all.21 = bf16[8,128,768]{2,1,0:T(8,128)(2,1)S(1)} all-to-all(bf16[8,128,768]{2,1,0:T(8,128)(2,1)} %bitcast.187), channel_id=1, replica_groups=mesh['dp'=4,'expert'=8] {'expert'}, dimensions={0} | all-to-all | bytes 3145728 | tf_op jit(solution)/shard_map/all_to_all | solution.py:149
  285.9 16.4 %add_convert_fusion = bf16[1024,3072]{1,0:T(8,128)(2,1)} fusion(f32[1024,3072]{1,0:T(8,128)} %get-tuple-element.109, f32[1024,3072]{1,0:T(8,128)} %get-tuple-element.129, bf16[1024,768]{1,0:T(8,128)(2,1)S(1)} %bitcast.199, bf16[1,3072,768]{2,1,0:T(8,128)(2,1)} %param.38), kind=kOutput, calls=%fused_computation.15 | convolution fusion | flops 4875878400 | bytes 37748736 | tf_op jit(solution)/shard_map/rd,fd->rf/dot_general | solution.py:166
  302.3 9.5 fusion.54
  316.3 21.0 %all-to-all-done.3 = bf16[8,128,768]{2,1,0:T(8,128)(2,1)} async-done(((bf16[8,128,768]{2,1,0:T(8,128)(2,1)}), bf16[8,128,768]{2,1,0:T(8,128)(2,1)}, u32[]{:S(2)}, u32[]{:S(2)}) %all-to-all-start.3) | async-done | bytes 1572896 | tf_op jit(solution)/shard_map/all_to_all | solution.py:182
  385.8 17.8 %multiply_reduce_fusion = (f32[12,512]{1,0:T(8,128)}, f32[12,512,1024]{2,1,0:T(8,128)}) fusion(f32[12,512,1024]{2,1,0:T(8,128)} %get-tuple-element.123, f32[12,512]{1,0:T(8,128)} %get-tuple-element.122, bf16[1024,12,64]{0,2,1:T(8,128)(2,1)} %bitcast.194, bf16[1,1024,12,64]{1,3,2,0:T(8,128)(2,1)} %bitcast.215), kind=kOutput, calls=%fused_computation.7 | convolution fusion | flops 824174592 | bytes 52748288 | tf_op jit(solution)/shard_map/sqhd,skhd->shqk/dot_general | solution.py:214
  403.6 10.6 %fusion.42 = bf16[1,1024,12,64]{1,3,2,0:T(8,128)(2,1)S(1)} fusion(f32[1,512,12,64]{1,3,2,0:T(8,128)} %fusion.60, bf16[1,1024,12,64]{1,3,2,0:T(8,128)(2,1)} %bitcast.216, f32[12,512,1024]{2,1,0:T(8,128)} %get-tuple-element.123, f32[12,512]{1,0:T(8,128)} %get-tuple-element.122), kind=kOutput, calls=%fused_computation.81 | convolution fusion | flops 819462144 | bytes 29130752 | tf_op jit(solution)/shard_map/shqk,sqhd->skhd/dot_general | solution.py:235
  414.3 21.8 %multiply_convert_fusion = bf16[12,512,1024]{2,1,0:T(8,128)(2,1)} fusion(f32[12,512,1024]{2,1,0:T(8,128)} %get-tuple-element.133, f32[12,512]{1,0:T(8,128)S(1)} %copy-done.52, f32[12,512,1024]{2,1,0:T(8,128)} %get-tuple-element.123, f32[12,512]{1,0:T(8,128)S(1)} %copy-done.51), kind=kLoop, calls=%fused_computation.6 | loop fusion | flops 25165824 | bytes 62963712 | tf_op jit(solution)/shard_map/convert_element_type | solution.py:218
  436.1 8.6 fusion.77
  461.4 9.1 convolution_convert_fusion.1
  470.6 9.4 convolution_convert_fusion.2
  480.1 119.1 %all-reduce.7.cloned.1.call-done = (f32[768,2304]{1,0:T(8,128)}, f32[768,768]{1,0:T(8,128)}) async-done(((f32[768,2304]{1,0:T(8,128)}, f32[768,768]{1,0:T(8,128)}), (f32[768,2304]{1,0:T(8,128)}, f32[768,768]{1,0:T(8,128)})) %all-reduce.7.cloned.1.call-update) | async-done | bytes 9437200 | tf_op jit(solution)/shard_map/psum | solution.py:14
  603.6 7.9 fusion.123
  627.6 23.4 %psum.46 = f32[768,4]{0,1:T(4,128)} all-reduce(f32[768,4]{0,1:T(4,128)S(1)} %pad_maximum_fusion.5), channel_id=1, replica_groups=mesh['dp'=4,'expert'=8] {'expert'}, use_global_device_ids=true, to_apply=%region_29.31 | all-reduce | flops 3072 | bytes 24576 | tf_op jit(solution)/shard_map/psum | solution.py:14
  651.0 20.8 %psum.47 = f32[768,4]{0,1:T(4,128)S(1)} all-reduce(f32[768,4]{0,1:T(4,128)} %psum.46), channel_id=1, replica_groups=mesh['dp'=4,'expert'=8] {'dp'}, use_global_device_ids=true, to_apply=%region_30.32 | all-reduce | flops 3072 | bytes 24576 | tf_op jit(solution)/shard_map/psum | solution.py:15
  678.3 293.6 %all-reduce.9.cloned.1.call-done = (f32[768,2304]{1,0:T(8,128)}, f32[768,768]{1,0:T(8,128)}) async-done(((f32[768,2304]{1,0:T(8,128)}, f32[768,768]{1,0:T(8,128)}), (f32[768,2304]{1,0:T(8,128)}, f32[768,768]{1,0:T(8,128)})) %all-reduce.9.cloned.1.call-update) | async-done | bytes 9437200 | tf_op jit(solution)/shard_map/psum | solution.py:15
  (241 shorter events, 185.5 us)
Async XLA Ops:
  8.0 19.3 %copy-start = (bf16[768,2304]{1,0:T(8,128)(2,1)S(1)}, bf16[768,2304]{1,0:T(8,128)(2,1)}, u32[]{:S(2)}) copy-start(bf16[768,2304]{1,0:T(8,128)(2,1)} %param.31) | copy-start | bytes 10616836
  9.9 108.6 %copy-start.56 = (f32[1024]{0:T(1024)}, f32[1024]{0:T(1024)S(1)}, u32[]{:S(2)}) copy-start(f32[1024]{0:T(1024)S(1)} %fusion.106) | copy-start | bytes 12292
  24.8 6.9 copy-start.30
  132.0 69.4 %copy-start.58 = (s32[1024]{0:T(1024)}, s32[1024]{0:T(1024)S(1)}, u32[]{:S(2)}) copy-start(s32[1024]{0:T(1024)S(1)} %get-tuple-element.107) | copy-start | bytes 12292
  165.7 35.7 %copy-start.21 = (bf16[8,128,768]{2,1,0:T(8,128)(2,1)}, bf16[8,128,768]{2,1,0:T(8,128)(2,1)S(1)}, u32[]{:S(2)}) copy-start(bf16[8,128,768]{2,1,0:T(8,128)(2,1)S(1)} %all_to_all.20) | copy-start | bytes 4718596
  201.4 10.7 %copy-start.72 = (bf16[1024,3072]{1,0:T(8,128)(2,1)}, bf16[1024,3072]{1,0:T(8,128)(2,1)S(1)}, u32[]{:S(2)}) copy-start(bf16[1024,3072]{1,0:T(8,128)(2,1)S(1)} %get-tuple-element.108) | copy-start | bytes 18874372
  212.1 6.9 copy-start.59
  212.1 6.9 copy-start.45
  212.1 25.4 %all-to-all-start.1 = ((bf16[8,128,768]{2,1,0:T(8,128)(2,1)}), bf16[8,128,768]{2,1,0:T(8,128)(2,1)}, u32[]{:S(2)}, u32[]{:S(2)}) async-start(bf16[8,128,768]{2,1,0:T(8,128)(2,1)} %bitcast.204), calls=%async_computation.1 | async-start | bytes 3145728 | tf_op jit(solution)/shard_map/all_to_all | solution.py:129
  219.1 28.2 %copy-start.48 = (f32[1024]{0:T(1024)}, f32[1024]{0:T(1024)S(1)}, u32[]{:S(2)}) copy-start(f32[1024]{0:T(1024)S(1)} %broadcast_select_fusion.1) | copy-start | bytes 12292
  285.9 16.4 %copy-start.26 = (bf16[8,128,768]{2,1,0:T(8,128)(2,1)}, bf16[8,128,768]{2,1,0:T(8,128)(2,1)S(1)}, u32[]{:S(2)}) copy-start(bf16[8,128,768]{2,1,0:T(8,128)(2,1)S(1)} %all_to_all.21) | copy-start | bytes 4718596
  311.8 25.5 %all-to-all-start.3 = ((bf16[8,128,768]{2,1,0:T(8,128)(2,1)}), bf16[8,128,768]{2,1,0:T(8,128)(2,1)}, u32[]{:S(2)}, u32[]{:S(2)}) async-start(bf16[8,128,768]{2,1,0:T(8,128)(2,1)} %bitcast.203), calls=%async_computation.3 | async-start | bytes 3145728 | tf_op jit(solution)/shard_map/all_to_all | solution.py:182
  316.2 283.0 %all-reduce.7.cloned.1.call-start = ((), (), s32[]{:S(2)}) async-start(), calls=%async_computation.8 | async-start | bytes 18874368 | tf_op jit(solution)/shard_map/psum | solution.py:14
  373.7 6.9 copy-start.8
  403.6 10.6 %copy-start.51 = (f32[12,512]{1,0:T(8,128)S(1)}, f32[12,512]{1,0:T(8,128)}, u32[]{:S(2)}) copy-start(f32[12,512]{1,0:T(8,128)} %get-tuple-element.122) | copy-start | bytes 73732
  403.6 10.6 %copy-start.52 = (f32[12,512]{1,0:T(8,128)S(1)}, f32[12,512]{1,0:T(8,128)}, u32[]{:S(2)}) copy-start(f32[12,512]{1,0:T(8,128)} %get-tuple-element.132) | copy-start | bytes 73732
  414.2 37.8 %copy-start.70 = (bf16[1,1024,12,64]{1,3,2,0:T(8,128)(2,1)}, bf16[1,1024,12,64]{1,3,2,0:T(8,128)(2,1)S(1)}, u32[]{:S(2)}) copy-start(bf16[1,1024,12,64]{1,3,2,0:T(8,128)(2,1)S(1)} %fusion.42) | copy-start | bytes 4718596
  414.2 21.9 %copy-start.9 = (bf16[1024,768]{0,1:T(8,128)(2,1)S(1)}, bf16[1024,768]{0,1:T(8,128)(2,1)}, u32[]{:S(2)}) copy-start(bf16[1024,768]{0,1:T(8,128)(2,1)} %copy.46) | copy-start | bytes 4718596
  436.1 8.7 copy-start.16
  436.1 8.7 copy-start.18
  444.8 7.0 copy-start.20
  461.4 211.0 %reduce-scatter.5.cloned.1.call-start = ((), (), s32[]{:S(2)}) async-start(), calls=%async_computation.7 | async-start | bytes 5898240 | tf_op jit(solution)/shard_map/reduce_scatter | solution.py:158
  470.6 204.7 %reduce-scatter.3.cloned.1.call-start = ((), (), s32[]{:S(2)}) async-start(), calls=%async_computation.6 | async-start | bytes 5898240 | tf_op jit(solution)/shard_map/reduce_scatter | solution.py:171
  480.1 491.8 %all-reduce.9.cloned.1.call-start = ((), (), s32[]{:S(2)}) async-start(), calls=%async_computation.9 | async-start | bytes 18874368 | tf_op jit(solution)/shard_map/psum | solution.py:15
  (58 other events, 201.2 us)
Sparse Core Ops, SparseCore 0:
  461.5 137.6 all-reduce.6
Sparse Core Ops, SparseCore 1:
  470.7 84.5 reduce-scatter.4
  557.4 85.6 reduce-scatter.2
  645.8 326.0 all-reduce.8
